TPU v7x, 128 devices: a whole 4x4x4 slice. The times are simulated.
128 devices in a mesh: layer: 4 (over z), row: 32 (over y, x, core).
Axes of the slice: x: 4, y: 4, z: 4, core: 2. Of those that a mesh axis runs over, the one named last changes fastest.
Arguments:
- rhs_sub: float32 [4, 3, 4096, 256], P('layer', None, 'row'), may hold values from -6 to 6
- rhs_root: float32 [2048, 256], P('row'), may hold values from -6 to 6
- lower_inv: float32 [4, 3, 4096, 4096], P('layer', None, 'row'), may hold values from -0.09375 to 0.09375
- upper_inv: float32 [4, 3, 4096, 4096], P('layer', None, 'row'), may hold values from -0.09375 to 0.09375
- coupling_low: float32 [4, 3, 2048, 4096], P('layer', None, None, 'row'), may hold values from -0.0390625 to 0.0390625
- coupling_up: float32 [4, 3, 4096, 2048], P('layer', None, 'row'), may hold values from -0.1875 to 0.1875
- tile_mask: int32 [4, 3, 16, 32], P('layer', None, None, 'row'), may hold values 0 or 1
- root_inv: float32 [2048, 2048], P('row'), may hold values from -0.125 to 0.125
Outputs:
- sol_sub: float32 [4, 3, 4096, 256], P('layer', None, 'row')
- sol_root: float32 [2048, 256], P('row')
All inputs are finite; a program needn't handle non-finite values. No bound on the sum of `tile_mask` on one device may be relied on, other than what follows from the above.
Results may differ from a plain program's by a relative error of at most 0.0001.
Values sent between devices are 32-bit elements; how exact they have to be, the bound alone decides.
No kernel may reach another device: no remote copies, remote signals or barrier semaphores. Data moves between devices by JAX's collectives and lax.ppermute only.
A program may use at most 128 MiB of HBM per device.

v0:
```python
import jax
import jax.numpy as jnp
from jax import lax
from jax.sharding import PartitionSpec as P

TILE = 128


def masked_tiles(coupling, pattern, tile, flipped):
    blocks, height, breadth = coupling.shape
    shaped = coupling.reshape(blocks, height // tile, tile, breadth // tile, tile)
    if flipped:
        pattern = jnp.transpose(pattern, (0, 2, 1))
    weights = pattern.astype(jnp.float32)[:, :, None, :, None]
    return (shaped * weights).reshape(blocks, height, breadth)


def fold_single(matrix, piece):
    return jnp.dot(
        matrix, piece, precision=lax.Precision.HIGHEST, preferred_element_type=jnp.float32
    )


def body(rhs_sub, rhs_root, lower_inv, upper_inv, coupling_low, coupling_up, tile_mask, root_inv):
    highest = lax.Precision.HIGHEST
    lower = lower_inv[0]
    upper = upper_inv[0]
    vectors = rhs_sub[0]
    blocks = vectors.shape[0]
    results = []
    for index in range(blocks):
        results.append(
            fold_single(lower[index], lax.all_gather(vectors[index], "row", axis=0, tiled=True))
        )
    interim = jnp.stack(results)
    lower_coupling = masked_tiles(coupling_low[0], tile_mask[0], TILE, False)
    local_part = lax.psum_scatter(
        jnp.einsum("kas,ksr->ar", lower_coupling, interim, precision=highest),
        "row",
        scatter_dimension=0,
        tiled=True,
    )
    layer_total = lax.psum(local_part, "layer")
    reduced = rhs_root - layer_total
    columns = root_inv
    sol_root = jnp.dot(
        columns,
        lax.all_gather(reduced, "row", axis=0, tiled=True),
        precision=highest,
        preferred_element_type=jnp.float32,
    )
    upper_coupling = masked_tiles(coupling_up[0], tile_mask[0], TILE, True)
    columns = upper_coupling
    coupled = jnp.einsum(
        "ksa,ar->ksr",
        columns,
        lax.all_gather(sol_root, "row", axis=0, tiled=True),
        precision=highest,
    )
    residue = interim - coupled
    outputs = []
    for index in range(blocks):
        outputs.append(
            fold_single(upper[index], lax.all_gather(residue[index], "row", axis=0, tiled=True))
        )
    solved = jnp.stack(outputs)
    return (solved[None], sol_root)


def solution(mesh):
    return jax.shard_map(
        body,
        mesh=mesh,
        in_specs=(
            P("layer", None, "row", None),
            P("row", None),
            P("layer", None, "row", None),
            P("layer", None, "row", None),
            P("layer", None, None, "row"),
            P("layer", None, "row", None),
            P("layer", None, None, "row"),
            P("row", None),
        ),
        out_specs=(P("layer", None, "row", None), P("row", None)),
        check_vma=False,
    )
```

profile of v0, /device:TPU:1, one launch (start us, length us, event | category | flops | bytes accessed | tf_op | source)
XLA Modules:
  0.0 543.6 jit_solution(12536181070227293686)
XLA Ops:
  7.2 1.8 fusion.65
  9.1 0.0 all-gather.23.cloned.1.call-start
  9.1 0.7 all-gather.23.cloned.1.call-update
  9.9 0.7 all-gather.21.cloned.1.call-update
  10.6 0.7 convert_element_type.19
  11.3 0.1 broadcast_bitcast_fusion
  11.4 48.9 %all-gather.19.cloned.1.call-done = f32[1,1,4096,256]{3,2,1,0:T(8,128)} async-done(((f32[1,1,128,256]{3,2,1,0:T(8,128)}), f32[1,1,4096,256]{3,2,1,0:T(8,128)}) %all-gather.19.cloned.1.call-update) | async-done | bytes 4194320 | tf_op jit(solution)/shard_map/all_gather | solution.py:33
  60.3 4.9 fusion.33
  65.3 42.7 %all-gather.23.cloned.1.call-done = f32[1,1,4096,256]{3,2,1,0:T(8,128)} async-done(((f32[1,1,128,256]{3,2,1,0:T(8,128)}), f32[1,1,4096,256]{3,2,1,0:T(8,128)}) %all-gather.23.cloned.1.call-update) | async-done | bytes 4194320 | tf_op jit(solution)/shard_map/all_gather | solution.py:33
  108.0 4.9 fusion.43
  112.9 42.7 %all-gather.21.cloned.1.call-done = f32[1,1,4096,256]{3,2,1,0:T(8,128)} async-done(((f32[1,1,128,256]{3,2,1,0:T(8,128)}), f32[1,1,4096,256]{3,2,1,0:T(8,128)}) %all-gather.21.cloned.1.call-update) | async-done | bytes 4194320 | tf_op jit(solution)/shard_map/all_gather | solution.py:33
  155.6 5.1 fusion.38
  160.7 5.1 fusion.14
  165.8 76.2 %reduce-scatter.2.cloned.1.call-done = f32[64,256]{1,0:T(8,128)} async-done(((f32[2048,256]{1,0:T(8,128)}), f32[64,256]{1,0:T(8,128)}) %reduce-scatter.2.cloned.1.call-update) | async-done | bytes 65552 | tf_op jit(solution)/shard_map/reduce_scatter | solution.py:37
  242.1 42.6 %all-reduce.2.cloned.1.call-done = f32[64,256]{1,0:T(8,128)} async-done(((f32[64,256]{1,0:T(8,128)}), f32[64,256]{1,0:T(8,128)}) %all-reduce.2.cloned.1.call-update) | async-done | bytes 65552 | tf_op jit(solution)/shard_map/psum | solution.py:43
  284.8 1.5 sub.6
  286.3 0.2 all-gather.17.cloned.1.call-start
  286.5 47.1 %all-gather.15.cloned.1.call-done = f32[2048,256]{1,0:T(8,128)} async-done(((f32[64,256]{1,0:T(8,128)}), f32[2048,256]{1,0:T(8,128)}) %all-gather.15.cloned.1.call-update) | async-done | bytes 2097168 | tf_op jit(solution)/shard_map/all_gather | solution.py:48
  333.6 3.6 convolution_bitcast_fusion
  337.2 0.0 all-gather.25.cloned.1.call-start
  337.2 42.9 %all-gather.17.cloned.1.call-done = f32[2048,256]{1,0:T(8,128)} async-done(((f32[64,256]{1,0:T(8,128)}), f32[2048,256]{1,0:T(8,128)}) %all-gather.17.cloned.1.call-update) | async-done | bytes 2097168 | tf_op jit(solution)/shard_map/all_gather | solution.py:57
  380.1 5.3 fusion.30
  385.4 0.8 fusion.64
  386.2 0.7 all-gather.29.cloned.1.call-update
  386.9 0.5 all-gather.27.cloned.1.call-update
  387.5 44.1 %all-gather.25.cloned.1.call-done = f32[1,4096,256]{2,1,0:T(8,128)} async-done(((f32[1,128,256]{2,1,0:T(8,128)}), f32[1,4096,256]{2,1,0:T(8,128)}) %all-gather.25.cloned.1.call-update) | async-done | bytes 4194320 | tf_op jit(solution)/shard_map/all_gather | solution.py:64
  431.5 9.2 %fusion.48 = f32[1,128,256]{1,2,0:T(8,128)S(1)} fusion(f32[1,3,128,4096]{3,2,1,0:T(8,128)} %param.11, f32[1,4096,256]{2,1,0:T(8,128)} %all-gather.25.cloned.1.call-done), kind=kOutput, calls=%fused_computation.36 | convolution fusion | flops 1610612736 | bytes 6422528 | tf_op jit(solution)/shard_map/dot_general | solution.py:19
  440.7 38.4 %all-gather.29.cloned.1.call-done = f32[1,4096,256]{2,1,0:T(8,128)} async-done(((f32[1,128,256]{2,1,0:T(8,128)}), f32[1,4096,256]{2,1,0:T(8,128)}) %all-gather.29.cloned.1.call-update) | async-done | bytes 4194320 | tf_op jit(solution)/shard_map/all_gather | solution.py:64
  479.2 9.2 %fusion.58 = f32[1,128,256]{1,2,0:T(8,128)S(1)} fusion(f32[1,3,128,4096]{3,2,1,0:T(8,128)} %param.11, f32[1,4096,256]{2,1,0:T(8,128)} %all-gather.29.cloned.1.call-done), kind=kOutput, calls=%fused_computation.38 | convolution fusion | flops 1610612736 | bytes 6422528 | tf_op jit(solution)/shard_map/dot_general | solution.py:19
  488.4 38.3 %all-gather.27.cloned.1.call-done = f32[1,4096,256]{2,1,0:T(8,128)} async-done(((f32[1,128,256]{2,1,0:T(8,128)}), f32[1,4096,256]{2,1,0:T(8,128)}) %all-gather.27.cloned.1.call-update) | async-done | bytes 4194320 | tf_op jit(solution)/shard_map/all_gather | solution.py:64
  526.6 9.2 %fusion.53 = f32[1,128,256]{1,2,0:T(8,128)S(1)} fusion(f32[1,3,128,4096]{3,2,1,0:T(8,128)} %param.11, f32[1,4096,256]{2,1,0:T(8,128)} %all-gather.27.cloned.1.call-done), kind=kOutput, calls=%fused_computation.37 | convolution fusion | flops 1610612736 | bytes 6422528 | tf_op jit(solution)/shard_map/dot_general | solution.py:19
  535.9 0.9 copy.10
  (22 shorter events, 0.4 us)
Async XLA Ops:
  7.2 326.4 %copy-start = (f32[64,2048]{1,0:T(8,128)S(1)}, f32[64,2048]{1,0:T(8,128)}, u32[]{:S(2)}) copy-start(f32[64,2048]{1,0:T(8,128)} %param.15) | copy-start | bytes 1572868
  7.2 53.2 %all-gather.19.cloned.1.call-start = ((), (), s32[]{:S(2)}) async-start(), calls=%async_computation.5 | async-start | bytes 4325376 | tf_op jit(solution)/shard_map/all_gather | solution.py:33
  9.1 98.9 %all-gather.23.cloned.1.call-start = ((), (), s32[]{:S(2)}) async-start(), calls=%async_computation.7 | async-start | bytes 4325376 | tf_op jit(solution)/shard_map/all_gather | solution.py:33
  9.8 145.7 %all-gather.21.cloned.1.call-start = ((), (), s32[]{:S(2)}) async-start(), calls=%async_computation.6 | async-start | bytes 4325376 | tf_op jit(solution)/shard_map/all_gather | solution.py:33
  10.6 231.5 %reduce-scatter.2.cloned.1.call-start = ((), (), s32[]{:S(2)}) async-start(), calls=%async_computation.1 | async-start | bytes 2162688 | tf_op jit(solution)/shard_map/reduce_scatter | solution.py:37
  155.6 5.1 copy-start.1
  160.6 124.1 %copy-start.2 = (f32[64,256]{1,0:T(8,128)S(1)}, f32[64,256]{1,0:T(8,128)}, u32[]{:S(2)}) copy-start(f32[64,256]{1,0:T(8,128)} %param.9) | copy-start | bytes 196612
  165.8 119.0 %all-reduce.2.cloned.1.call-start = ((), (), s32[]{:S(2)}) async-start(), calls=%async_computation.2 | async-start | bytes 131072 | tf_op jit(solution)/shard_map/psum | solution.py:43
  242.1 91.5 %all-gather.15.cloned.1.call-start = ((), (), s32[]{:S(2)}) async-start(), calls=%async_computation.3 | async-start | bytes 2162688 | tf_op jit(solution)/shard_map/all_gather | solution.py:48
  286.3 93.8 %all-gather.17.cloned.1.call-start = ((), (), s32[]{:S(2)}) async-start(), calls=%async_computation.4 | async-start | bytes 2162688 | tf_op jit(solution)/shard_map/all_gather | solution.py:57
  337.2 94.4 %all-gather.25.cloned.1.call-start = ((), (), s32[]{:S(2)}) async-start(), calls=%async_computation.8 | async-start | bytes 4325376 | tf_op jit(solution)/shard_map/all_gather | solution.py:64
  386.1 93.0 %all-gather.29.cloned.1.call-start = ((), (), s32[]{:S(2)}) async-start(), calls=%async_computation.10 | async-start | bytes 4325376 | tf_op jit(solution)/shard_map/all_gather | solution.py:64
  386.9 139.8 %all-gather.27.cloned.1.call-start = ((), (), s32[]{:S(2)}) async-start(), calls=%async_computation.9 | async-start | bytes 4325376 | tf_op jit(solution)/shard_map/all_gather | solution.py:64
Sparse Core Ops, SparseCore 0:
  10.8 49.4 all-gather.18
  62.6 45.3 all-gather.22
  110.2 45.3 all-gather.20
  165.9 76.1 reduce-scatter.1
  244.2 40.5 all-reduce.1
  287.5 46.0 all-gather.14
  337.3 42.7 all-gather.16
  386.3 45.2 all-gather.24
  433.8 45.3 all-gather.28
  481.3 45.3 all-gather.26
where the time goes:
time: 544 us
  waiting for transfers between devices  467 us (86%)
  matrix products  56.3 us (10%)
  between operations  14.3 us (3%)
    all_gather x3, waiting for transfers between devices, body(): lax.all_gather(vectors[index], 'row', axis=0, tiled=True)  134 us
    all_gather x3, waiting for transfers between devices, body(): lax.all_gather(residue[index], 'row', axis=0, tiled=True)  121 us
    reduce_scatter x1, waiting for transfers between devices, body(): lax.psum_scatter(jnp.einsum('kas,ksr->ar', lower_coupling, interim, preci...  76.2 us
    all_gather x1, waiting for transfers between devices, body(): lax.all_gather(reduced, 'row', axis=0, tiled=True)  47.1 us
    all_gather x1, waiting for transfers between devices, body(): lax.all_gather(sol_root, 'row', axis=0, tiled=True)  42.9 us
    psum x1, waiting for transfers between devices, body(): layer_total = lax.psum(local_part, 'layer')  42.6 us
    dot_general x6, matrix products, fold_single(): jnp.dot(matrix, piece, precision=lax.Precision.HIGHEST, preferred_element...  42.4 us
  transfers between devices with their start and end apart: 10, of which 10 were waited for; matrix products, arithmetic and copies ran while one was open for 5% of the time, Pallas kernels for 0%

commit v1 on v0

--- a/solution.py
+++ b/solution.py
@@ -40,7 +40,7 @@
         scatter_dimension=0,
         tiled=True,
     )
-    layer_total = lax.psum(local_part, "layer")
+    layer_total = jnp.sum(lax.all_gather(local_part, "layer"), axis=0)
     reduced = rhs_root - layer_total
     columns = root_inv
     sol_root = jnp.dot(

time: 544 us -> 510 us (0.938)
  waiting for transfers between devices: 467 us -> 424 us
  blocking collectives: 0 us -> 10 us
    psum x1 -> x0, waiting for transfers between devices: 42.6 us -> none  [body(): layer_total = lax.psum(local_part, 'layer')]
    all_gather x0 -> x1, blocking collectives: none -> 10 us  [body(): layer_total = jnp.sum(lax.all_gather(local_part, 'layer'), axis=0)]
  transfers between devices with their start and end apart: 10 -> 9, of which waited for: 10 -> 9; matrix products, arithmetic and copies ran while one was open for 5% -> 6% of each run, Pallas kernels for 0% -> 0%
where the time goes in v1:
time: 510 us
  waiting for transfers between devices  424 us (83%)
  matrix products  56.3 us (11%)
  between operations  13.9 us (3%)
  blocking collectives  10 us (2%)
    all_gather x3, waiting for transfers between devices, body(): lax.all_gather(vectors[index], 'row', axis=0, tiled=True)  134 us
    all_gather x3, waiting for transfers between devices, body(): lax.all_gather(residue[index], 'row', axis=0, tiled=True)  121 us
    reduce_scatter x1, waiting for transfers between devices, body(): lax.psum_scatter(jnp.einsum('kas,ksr->ar', lower_coupling, interim, preci...  76.2 us
    all_gather x1, waiting for transfers between devices, body(): lax.all_gather(reduced, 'row', axis=0, tiled=True)  47.1 us
    all_gather x1, waiting for transfers between devices, body(): lax.all_gather(sol_root, 'row', axis=0, tiled=True)  42.9 us
    dot_general x6, matrix products, fold_single(): jnp.dot(matrix, piece, precision=lax.Precision.HIGHEST, preferred_element...  42.4 us
  transfers between devices with their start and end apart: 9, of which 9 were waited for; matrix products, arithmetic and copies ran while one was open for 6% of the time, Pallas kernels for 0%

profile of v1, /device:TPU:1, one launch (start us, length us, event | category | flops | bytes accessed | tf_op | source)
XLA Modules:
  0.0 510.0 jit_solution(12828090983109233515)
XLA Ops:
  7.2 1.8 fusion.65
  9.1 0.7 all-gather.24.cloned.1.call-update
  9.9 0.7 all-gather.22.cloned.1.call-update
  10.6 0.7 convert_element_type.19
  11.3 0.1 broadcast_bitcast_fusion
  11.4 48.9 %all-gather.20.cloned.1.call-done = f32[1,1,4096,256]{3,2,1,0:T(8,128)} async-done(((f32[1,1,128,256]{3,2,1,0:T(8,128)}), f32[1,1,4096,256]{3,2,1,0:T(8,128)}) %all-gather.20.cloned.1.call-update) | async-done | bytes 4194320 | tf_op jit(solution)/shard_map/all_gather | solution.py:33
  60.3 4.9 fusion.33
  65.3 42.7 %all-gather.24.cloned.1.call-done = f32[1,1,4096,256]{3,2,1,0:T(8,128)} async-done(((f32[1,1,128,256]{3,2,1,0:T(8,128)}), f32[1,1,4096,256]{3,2,1,0:T(8,128)}) %all-gather.24.cloned.1.call-update) | async-done | bytes 4194320 | tf_op jit(solution)/shard_map/all_gather | solution.py:33
  108.0 4.9 fusion.43
  112.9 42.7 %all-gather.22.cloned.1.call-done = f32[1,1,4096,256]{3,2,1,0:T(8,128)} async-done(((f32[1,1,128,256]{3,2,1,0:T(8,128)}), f32[1,1,4096,256]{3,2,1,0:T(8,128)}) %all-gather.22.cloned.1.call-update) | async-done | bytes 4194320 | tf_op jit(solution)/shard_map/all_gather | solution.py:33
  155.6 5.1 fusion.38
  160.7 5.1 fusion.14
  165.8 0.0 all-gather.16.cloned.1.call-start
  165.8 76.2 %reduce-scatter.2.cloned.1.call-done = f32[64,256]{1,0:T(8,128)} async-done(((f32[2048,256]{1,0:T(8,128)}), f32[64,256]{1,0:T(8,128)}) %reduce-scatter.2.cloned.1.call-update) | async-done | bytes 65552 | tf_op jit(solution)/shard_map/reduce_scatter | solution.py:37
  242.1 10.0 %all-gather.3 = f32[256,256]{1,0:T(8,128)S(1)} all-gather(f32[64,256]{1,0:T(8,128)} %reduce-scatter.2.cloned.1.call-done), channel_id=5, replica_groups=mesh['layer'=4,'row'=32] {'layer'}, dimensions={0}, use_global_device_ids=true | all-gather | bytes 327680 | tf_op jit(solution)/shard_map/all_gather | solution.py:43
  252.1 0.6 sub.6
  252.8 0.2 all-gather.18.cloned.1.call-start
  253.0 47.1 %all-gather.16.cloned.1.call-done = f32[2048,256]{1,0:T(8,128)} async-done(((f32[64,256]{1,0:T(8,128)}), f32[2048,256]{1,0:T(8,128)}) %all-gather.16.cloned.1.call-update) | async-done | bytes 2097168 | tf_op jit(solution)/shard_map/all_gather | solution.py:48
  300.1 3.6 convolution_bitcast_fusion
  303.7 0.0 all-gather.26.cloned.1.call-start
  303.7 42.9 %all-gather.18.cloned.1.call-done = f32[2048,256]{1,0:T(8,128)} async-done(((f32[64,256]{1,0:T(8,128)}), f32[2048,256]{1,0:T(8,128)}) %all-gather.18.cloned.1.call-update) | async-done | bytes 2097168 | tf_op jit(solution)/shard_map/all_gather | solution.py:57
  346.6 5.3 %fusion.30 = f32[3,128,256]{2,1,0:T(8,128)S(1)} fusion(f32[2048,256]{1,0:T(8,128)} %all-gather.18.cloned.1.call-done, f32[1,3,128,2048]{3,2,1,0:T(8,128)} %param.13, f32[3,2048]{1,0:T(4,128)S(1)} %bitcast.112, f32[1,128,256]{2,1,0:T(8,128)S(1)} %fusion.43, f32[1,128,256]{2,1,0:T(8,128)S(1)} %fusion.38, f32[1,128,256]{2,1,0:T(8,128)S(1)} %fusion.33), kind=kOutput, calls=%fused_computation.32 | convolution fusion | flops 2417000448 | bytes 6053888 | tf_op jit(solution)/shard_map/ksa,ar->ksr/dot_general | solution.py:54
  351.9 0.8 fusion.64
  352.7 0.7 all-gather.30.cloned.1.call-update
  353.5 0.7 all-gather.28.cloned.1.call-update
  354.1 43.9 %all-gather.26.cloned.1.call-done = f32[1,4096,256]{2,1,0:T(8,128)} async-done(((f32[1,128,256]{2,1,0:T(8,128)}), f32[1,4096,256]{2,1,0:T(8,128)}) %all-gather.26.cloned.1.call-update) | async-done | bytes 4194320 | tf_op jit(solution)/shard_map/all_gather | solution.py:64
  398.1 9.2 %fusion.48 = f32[1,128,256]{1,2,0:T(8,128)S(1)} fusion(f32[1,3,128,4096]{3,2,1,0:T(8,128)} %param.11, f32[1,4096,256]{2,1,0:T(8,128)} %all-gather.26.cloned.1.call-done), kind=kOutput, calls=%fused_computation.36 | convolution fusion | flops 1610612736 | bytes 6422528 | tf_op jit(solution)/shard_map/dot_general | solution.py:19
  407.2 38.4 %all-gather.30.cloned.1.call-done = f32[1,4096,256]{2,1,0:T(8,128)} async-done(((f32[1,128,256]{2,1,0:T(8,128)}), f32[1,4096,256]{2,1,0:T(8,128)}) %all-gather.30.cloned.1.call-update) | async-done | bytes 4194320 | tf_op jit(solution)/shard_map/all_gather | solution.py:64
  445.7 9.2 %fusion.58 = f32[1,128,256]{1,2,0:T(8,128)S(1)} fusion(f32[1,3,128,4096]{3,2,1,0:T(8,128)} %param.11, f32[1,4096,256]{2,1,0:T(8,128)} %all-gather.30.cloned.1.call-done), kind=kOutput, calls=%fused_computation.38 | convolution fusion | flops 1610612736 | bytes 6422528 | tf_op jit(solution)/shard_map/dot_general | solution.py:19
  454.9 38.4 %all-gather.28.cloned.1.call-done = f32[1,4096,256]{2,1,0:T(8,128)} async-done(((f32[1,128,256]{2,1,0:T(8,128)}), f32[1,4096,256]{2,1,0:T(8,128)}) %all-gather.28.cloned.1.call-update) | async-done | bytes 4194320 | tf_op jit(solution)/shard_map/all_gather | solution.py:64
  493.3 9.2 %fusion.53 = f32[1,128,256]{1,2,0:T(8,128)S(1)} fusion(f32[1,3,128,4096]{3,2,1,0:T(8,128)} %param.11, f32[1,4096,256]{2,1,0:T(8,128)} %all-gather.28.cloned.1.call-done), kind=kOutput, calls=%fused_computation.37 | convolution fusion | flops 1610612736 | bytes 6422528 | tf_op jit(solution)/shard_map/dot_general | solution.py:19
  502.5 0.9 copy.10
  (21 shorter events, 0.4 us)
Async XLA Ops:
  7.2 292.9 %copy-start = (f32[64,2048]{1,0:T(8,128)S(1)}, f32[64,2048]{1,0:T(8,128)}, u32[]{:S(2)}) copy-start(f32[64,2048]{1,0:T(8,128)} %param.15) | copy-start | bytes 1572868
  7.2 53.2 %all-gather.20.cloned.1.call-start = ((), (), s32[]{:S(2)}) async-start(), calls=%async_computation.4 | async-start | bytes 4325376 | tf_op jit(solution)/shard_map/all_gather | solution.py:33
  9.1 98.9 %all-gather.24.cloned.1.call-start = ((), (), s32[]{:S(2)}) async-start(), calls=%async_computation.6 | async-start | bytes 4325376 | tf_op jit(solution)/shard_map/all_gather | solution.py:33
  9.8 145.7 %all-gather.22.cloned.1.call-start = ((), (), s32[]{:S(2)}) async-start(), calls=%async_computation.5 | async-start | bytes 4325376 | tf_op jit(solution)/shard_map/all_gather | solution.py:33
  10.6 231.5 %reduce-scatter.2.cloned.1.call-start = ((), (), s32[]{:S(2)}) async-start(), calls=%async_computation.1 | async-start | bytes 2162688 | tf_op jit(solution)/shard_map/reduce_scatter | solution.py:37
  155.6 5.1 copy-start.1
  160.7 91.5 %copy-start.2 = (f32[64,256]{1,0:T(8,128)S(1)}, f32[64,256]{1,0:T(8,128)}, u32[]{:S(2)}) copy-start(f32[64,256]{1,0:T(8,128)} %param.9) | copy-start | bytes 196612
  165.8 134.3 %all-gather.16.cloned.1.call-start = ((), (), s32[]{:S(2)}) async-start(), calls=%async_computation.2 | async-start | bytes 2162688 | tf_op jit(solution)/shard_map/all_gather | solution.py:48
  252.8 93.8 %all-gather.18.cloned.1.call-start = ((), (), s32[]{:S(2)}) async-start(), calls=%async_computation.3 | async-start | bytes 2162688 | tf_op jit(solution)/shard_map/all_gather | solution.py:57
  303.7 94.4 %all-gather.26.cloned.1.call-start = ((), (), s32[]{:S(2)}) async-start(), calls=%async_computation.7 | async-start | bytes 4325376 | tf_op jit(solution)/shard_map/all_gather | solution.py:64
  352.7 93.0 %all-gather.30.cloned.1.call-start = ((), (), s32[]{:S(2)}) async-start(), calls=%async_computation.9 | async-start | bytes 4325376 | tf_op jit(solution)/shard_map/all_gather | solution.py:64
  353.4 139.9 %all-gather.28.cloned.1.call-start = ((), (), s32[]{:S(2)}) async-start(), calls=%async_computation.8 | async-start | bytes 4325376 | tf_op jit(solution)/shard_map/all_gather | solution.py:64
Sparse Core Ops, SparseCore 0:
  10.8 49.4 all-gather.19
  62.6 45.3 all-gather.23
  110.2 45.3 all-gather.21
  165.9 76.1 reduce-scatter.1
  252.9 47.1 all-gather.15
  303.8 42.7 all-gather.17
  352.8 45.2 all-gather.25
  400.3 45.3 all-gather.29
  447.9 45.3 all-gather.27
